TPU v7x, 128 devices: a whole 4x4x4 slice. The times are simulated.
128 devices in a mesh: ctx: 32 (over z_lo, y, x), head: 4 (over z_hi, core).
Axes of the slice: x: 4, y: 4, z: 4 (z_hi: 2, z_lo: 2; z = z_hi * 2 + z_lo), core: 2. Of those that a mesh axis runs over, the one named last changes fastest.
Arguments:
- queries: bfloat16 [1024, 16384], P('ctx', 'head'), may hold values from -512 to 512
- kv_cache: bfloat16 [2, 16384, 1024], P(None, 'ctx', 'head'), may hold values from -7 to 7
- fill_len: int32 [32], P('ctx'), may hold values from 64 to 512
- prompt_offset: int32 [1], replicated, may hold values from 8192 to 15360
Outputs:
- attended: bfloat16 [1024, 16384], P(('ctx', 'head'))
All inputs are finite; a program needn't handle non-finite values.
Results may differ from a plain program's by a relative error of at most 0.0045.
Values may be sent and summed in bfloat16 or wider, within the bound.
No kernel may reach another device: no remote copies, remote signals or barrier semaphores. Data moves between devices by JAX's collectives and lax.ppermute only.
A program may use at most 192 MiB of HBM per device.

v0:
```python
import math
import jax
import jax.numpy as jnp
from jax import lax
from jax.sharding import PartitionSpec as P

HEAD_DIM = 128


def shard_partial(query_rows, key_block, value_block, allowed):
    scaling = 1.0 / math.sqrt(query_rows.shape[-1])
    scores = (
        jnp.einsum("nhgd,khd->hgnk", query_rows, key_block, preferred_element_type=jnp.float32)
        * scaling
    )
    scores = jnp.where(allowed[None, None], scores, -1e30)
    row_max = jnp.max(scores, axis=-1)
    weights = jnp.exp(scores - row_max[..., None])
    row_sum = jnp.sum(weights, axis=-1)
    rounded = weights.astype(jnp.bfloat16)
    weighted = jnp.einsum(
        "hgnk,khd->nhgd", rounded, value_block, preferred_element_type=jnp.float32
    )
    weighted = weighted / jnp.transpose(row_sum, (2, 0, 1))[..., None]
    row_count = query_rows.shape[0]
    partial_value = weighted.astype(jnp.bfloat16).reshape(row_count, -1)
    log_total = jnp.transpose(row_max + jnp.log(row_sum), (2, 0, 1)).reshape(row_count, -1)
    return (partial_value, log_total)


def per_device(queries, kv_cache, fill_len, prompt_offset):
    ctx_size = lax.axis_size("ctx")
    ctx_rank = lax.axis_index("ctx")
    slots = kv_cache.shape[1]
    kv_local = kv_cache.shape[2] // HEAD_DIM
    feat_width = queries.shape[1]
    heads_local = feat_width // HEAD_DIM
    groups = heads_local // kv_local
    slot_ids = jnp.arange(slots, dtype=jnp.int32)
    start_pos = prompt_offset[0]
    key_block = kv_cache[0].reshape(slots, kv_local, HEAD_DIM)
    value_block = kv_cache[1].reshape(slots, kv_local, HEAD_DIM)
    key_pos = ctx_rank * slots + slot_ids
    live_slots = slot_ids < fill_len[0]
    arrived = lax.all_gather(queries, "ctx", axis=0, tiled=True)
    row_count = arrived.shape[0]
    query_pos = start_pos + jnp.arange(row_count, dtype=jnp.int32)
    allowed = live_slots[None, :] & (key_pos[None, :] <= query_pos[:, None])
    partial_value, log_total = shard_partial(
        arrived.reshape(row_count, kv_local, groups, HEAD_DIM), key_block, value_block, allowed
    )
    received = lax.all_to_all(
        partial_value[None], ("ctx", "head"), split_axis=1, concat_axis=0, tiled=True
    )
    received_logs = lax.all_to_all(
        log_total[None], ("ctx", "head"), split_axis=1, concat_axis=0, tiled=True
    )
    head_size = lax.axis_size("head")
    token_rows = received.shape[1]
    received = received.reshape(ctx_size, head_size, token_rows, heads_local, HEAD_DIM)
    received_logs = received_logs.reshape(ctx_size, head_size, token_rows, heads_local)
    log_peak = jnp.max(received_logs, axis=0)
    shares = jnp.exp(received_logs - log_peak[None])
    merged = (
        jnp.sum(shares[..., None] * received.astype(jnp.float32), axis=0)
        / jnp.sum(shares, axis=0)[..., None]
    )
    merged = jnp.transpose(merged, (1, 0, 2, 3)).reshape(token_rows, head_size * feat_width)
    return merged.astype(jnp.bfloat16)


def solution(mesh):
    in_specs = (P("ctx", "head"), P(None, "ctx", "head"), P("ctx"), P())
    out_specs = P(("ctx", "head"), None)
    return jax.shard_map(
        per_device, mesh=mesh, in_specs=in_specs, out_specs=out_specs, check_vma=False
    )
```

profile of v0, /device:TPU:12, one launch (start us, length us, event | category | flops | bytes accessed | tf_op | source)
XLA Modules:
  0.0 589.1 jit_solution(6618123651662183194)
XLA Ops:
  6.5 0.0 all-gather.2.cloned.1.call-start
  6.5 0.7 all-gather.2.cloned.1.call-update
  8.5 1.1 fusion.13
  9.6 0.1 copy.46
  9.8 0.1 copy.36
  9.9 0.4 compare_and_fusion
  10.4 158.9 %all-gather.2.cloned.1.call-done = bf16[1024,4096]{1,0:T(8,128)(2,1)} async-done(((bf16[32,4096]{1,0:T(8,128)(2,1)}), bf16[1024,4096]{1,0:T(8,128)(2,1)}) %all-gather.2.cloned.1.call-update) | async-done | bytes 8388624 | tf_op jit(solution)/shard_map/all_gather | solution.py:45
  169.3 12.0 %copy.32 = bf16[1024,4096]{0,1:T(8,128)(2,1)} copy(bf16[1024,4096]{1,0:T(8,128)(2,1)} %all-gather.2.cloned.1.call-done) | data formatting | bytes 16777216 | tf_op jit(solution)/shard_map/all_gather | solution.py:45
  181.3 28.0 %fusion.2 = (f32[2,16,1024]{2,1,0:T(8,128)S(1)}, f32[2,512,1024,16]{2,1,3,0:T(8,128)}) fusion(pred[1024,512]{0,1:T(8,128)(4,1)S(1)} %compare_and_fusion, bf16[512,2,128,1]{0,2,3,1:T(8,128)(2,1)S(1)} %bitcast.63, bf16[1024,2,16,128]{0,3,2,1:T(8,128)(2,1)} %bitcast.58), kind=kOutput, calls=%fused_computation.4 | convolution fusion | flops 4345266176 | bytes 76414976 | tf_op jit(solution)/shard_map/nhgd,khd->hgnk/dot_general | solution.py:13
  209.3 21.6 %fusion.1 = f32[2,16,1024]{2,1,0:T(8,128)S(1)} fusion(f32[2,512,1024,16]{2,1,3,0:T(8,128)} %get-tuple-element.10, f32[2,16,1024]{2,1,0:T(8,128)S(1)} %get-tuple-element.9, pred[1024,512]{0,1:T(8,128)(4,1)S(1)} %compare_and_fusion), kind=kLoop, calls=%fused_computation.3 | loop fusion | flops 67076096 | bytes 67895296 | tf_op jit(solution)/shard_map/reduce_sum | solution.py:19
  230.9 0.3 copy.35
  231.3 0.6 broadcast.68
  231.8 1.9 reduce.1
  233.8 0.9 reshape.98
  234.7 16.7 %all-to-all-start = ((f32[128,1,256]{2,1,0:T(1,128)}), f32[128,1,256]{2,1,0:T(1,128)S(1)}, u32[]{:S(2)}, u32[]{:S(2)}) async-start(f32[128,1,256]{2,1,0:T(1,128)} %reshape.98), calls=%async_computation | async-start | bytes 262144 | tf_op jit(solution)/shard_map/all_to_all | solution.py:55
  251.4 28.0 %fusion.6 = bf16[1024,2,16,128]{0,3,2,1:T(8,128)(2,1)} fusion(f32[1024,2,16]{0,2,1:T(8,128)S(1)} %bitcast.65, bf16[512,2,128,1]{0,2,3,1:T(8,128)(2,1)S(1)} %bitcast.67, f32[2,512,1024,16]{2,1,3,0:T(8,128)} %get-tuple-element.10, f32[2,16,1024]{2,1,0:T(8,128)S(1)} %get-tuple-element.9, pred[1024,512]{0,1:T(8,128)(4,1)S(1)} %compare_and_fusion), kind=kOutput, calls=%fused_computation.8 | convolution fusion | flops 4370464768 | bytes 76546048 | tf_op jit(solution)/shard_map/hgnk,khd->nhgd/dot_general | solution.py:21
  279.5 36.5 %copy.38 = bf16[1,1024,4096]{2,0,1:T(2,128)(2,1)} copy(bf16[1,1024,4096]{1,2,0:T(8,128)(2,1)} %bitcast.59) | data formatting | bytes 16777216 | tf_op jit(solution)/shard_map/broadcast_in_dim;reshape | solution.py:53
  316.0 0.5 broadcast.67
  316.5 52.4 %reduce = bf16[1024,4096]{1,0:T(8,128)(2,1)} reduce(bf16[1024,1,4096]{2,1,0:T(2,128)(2,1)} %bitcast.56, bf16[]{:T(256)} %broadcast.67), dimensions={1}, to_apply=%bitcast.45.reduce_sub_computation | reduce | bytes 16777218
  369.0 15.7 %reshape.96 = bf16[128,2,16384]{2,1,0:T(2,128)(2,1)} reshape(bf16[1024,4096]{1,0:T(8,128)(2,1)} %reduce) | data formatting | bytes 16777216
  384.7 0.0 all-to-all-done
  384.7 10.2 %all-to-all-start.1 = ((bf16[128,2,16384]{2,1,0:T(2,128)(2,1)}), bf16[128,2,16384]{2,1,0:T(2,128)(2,1)}, u32[]{:S(2)}, u32[]{:S(2)}) async-start(bf16[128,2,16384]{2,1,0:T(2,128)(2,1)} %reshape.96), calls=%async_computation.1 | async-start | bytes 16777216 | tf_op jit(solution)/shard_map/all_to_all | solution.py:52
  394.9 0.9 reduce.2
  395.8 0.9 reshape.99
  396.8 0.1 reduce_max.22
  396.8 0.1 fusion.12
  396.9 121.9 %all-to-all-done.1 = bf16[128,2,16384]{2,1,0:T(2,128)(2,1)} async-done(((bf16[128,2,16384]{2,1,0:T(2,128)(2,1)}), bf16[128,2,16384]{2,1,0:T(2,128)(2,1)}, u32[]{:S(2)}, u32[]{:S(2)}) %all-to-all-start.1) | async-done | bytes 8388640 | tf_op jit(solution)/shard_map/all_to_all | solution.py:52
  518.8 38.4 %reshape.97 = bf16[1024,1,4096]{2,1,0:T(2,128)(2,1)} reshape(bf16[128,2,16384]{2,1,0:T(2,128)(2,1)} %all-to-all-done.1) | data formatting | bytes 16777216
  557.2 18.9 %bitcast_convert_fusion = f32[1,1024,4096]{2,0,1:T(1,128)S(1)} fusion(bf16[1024,1,4096]{2,1,0:T(2,128)(2,1)} %reshape.97), kind=kLoop, calls=%fused_computation.23 | loop fusion | flops 4194304 | bytes 25165824 | tf_op jit(solution)/shard_map/convert_element_type | solution.py:65
  576.1 5.1 multiply_reduce_fusion
  581.1 0.2 fusion.9
  581.4 0.9 copy.49
  (5 shorter events, 0.1 us)
Async XLA Ops:
  6.5 162.8 %all-gather.2.cloned.1.call-start = ((), (), s32[]{:S(2)}) async-start(), calls=%async_computation.2 | async-start | bytes 8650752 | tf_op jit(solution)/shard_map/all_gather | solution.py:45
  234.7 150.0 %all-to-all-start = ((f32[128,1,256]{2,1,0:T(1,128)}), f32[128,1,256]{2,1,0:T(1,128)S(1)}, u32[]{:S(2)}, u32[]{:S(2)}) async-start(f32[128,1,256]{2,1,0:T(1,128)} %reshape.98), calls=%async_computation | async-start | bytes 262144 | tf_op jit(solution)/shard_map/all_to_all | solution.py:55
  384.7 134.1 %all-to-all-start.1 = ((bf16[128,2,16384]{2,1,0:T(2,128)(2,1)}), bf16[128,2,16384]{2,1,0:T(2,128)(2,1)}, u32[]{:S(2)}, u32[]{:S(2)}) async-start(bf16[128,2,16384]{2,1,0:T(2,128)(2,1)} %reshape.96), calls=%async_computation.1 | async-start | bytes 16777216 | tf_op jit(solution)/shard_map/all_to_all | solution.py:52
Sparse Core Ops, SparseCore 0:
  9.0 160.2 all-gather.1
where the time goes:
time: 592 us; the launch traced here: 589 us
  waiting for transfers between devices  282 us (48%)
  local copies, waits for them, and re-layouts  108 us (18%)
  other arithmetic  102 us (17%)
  matrix products  56 us (9%)
  starting transfers between devices  27 us (5%)
  between operations  14.8 us (2%)
    all_gather x1, waiting for transfers between devices, per_device(): arrived = lax.all_gather(queries, 'ctx', axis=0, tiled=True)  159 us
    all_to_all x1, waiting for transfers between devices, per_device(): lax.all_to_all(partial_value[None], ('ctx', 'head'), split_axis=1, concat...  122 us
    unnamed x8, local copies, waits for them, and re-layouts  58 us
    unnamed x2, other arithmetic  54.4 us
    another operation x1, local copies, waits for them, and re-layouts, per_device(): partial_value[None]  36.5 us
    dot_general x1, matrix products, shard_partial(): jnp.einsum('hgnk,khd->nhgd', rounded, value_block, preferred_element_type...  28 us
    dot_general x1, matrix products, shard_partial(): jnp.einsum('nhgd,khd->hgnk', query_rows, key_block, preferred_element_typ...  28 us
    reduce_sum x1, other arithmetic, shard_partial(): row_sum = jnp.sum(weights, axis=-1)  21.6 us
  transfers between devices with their start and end apart: 3, of which 2 were waited for; matrix products, arithmetic and copies ran while one was open for 23% of the time, Pallas kernels for 0%

commit v1 on v0

--- a/solution.py
+++ b/solution.py
@@ -3,6 +3,7 @@
 import jax.numpy as jnp
 from jax import lax
 from jax.sharding import PartitionSpec as P
+from jax.lax import all_to_all, axis_size
 
 HEAD_DIM = 128
 
@@ -42,7 +43,9 @@
     value_block = kv_cache[1].reshape(slots, kv_local, HEAD_DIM)
     key_pos = ctx_rank * slots + slot_ids
     live_slots = slot_ids < fill_len[0]
-    arrived = lax.all_gather(queries, "ctx", axis=0, tiled=True)
+    arrived = jnp.concatenate(
+        all_to_all(jnp.stack([queries] * axis_size("ctx"), 0), "ctx", 0, 0), axis=0
+    )
     row_count = arrived.shape[0]
     query_pos = start_pos + jnp.arange(row_count, dtype=jnp.int32)
     allowed = live_slots[None, :] & (key_pos[None, :] <= query_pos[:, None])

time: 592 us -> 552 us (0.932)
  waiting for transfers between devices: 282 us -> 242 us
  between operations: 14.8 us -> 1.47 us
    all_gather x1 -> x0, waiting for transfers between devices: 159 us -> none  [per_device(): arrived = lax.all_gather(queries, 'ctx', axis=0, tiled=True)]
    all_to_all x0 -> x1, waiting for transfers between devices: none -> 120 us  [per_device(): all_to_all(jnp.stack([queries] * axis_size('ctx'), 0), 'ctx', 0, 0)]
    all_gather x1 -> x0, local copies, waits for them, and re-layouts: 12 us -> none  [per_device(): arrived = lax.all_gather(queries, 'ctx', axis=0, tiled=True)]
    unnamed x8 -> x11, local copies, waits for them, and re-layouts: 58 us -> 67.4 us
    all_to_all x0 -> x1, starting transfers between devices: none -> 8.89 us  [per_device(): all_to_all(jnp.stack([queries] * axis_size('ctx'), 0), 'ctx', 0, 0)]
  transfers between devices with their start and end apart: 3 -> 3, of which waited for: 2 -> 2; matrix products, arithmetic and copies ran while one was open for 23% -> 25% of each run, Pallas kernels for 0% -> 0%
where the time goes in v1:
time: 552 us; the launch traced here: 549 us
  waiting for transfers between devices  242 us (44%)
  local copies, waits for them, and re-layouts  110 us (20%)
  other arithmetic  102 us (18%)
  matrix products  61.7 us (11%)
  starting transfers between devices  32.6 us (6%)
    all_to_all x1, waiting for transfers between devices, per_device(): lax.all_to_all(partial_value[None], ('ctx', 'head'), split_axis=1, concat...  122 us
    all_to_all x1, waiting for transfers between devices, per_device(): all_to_all(jnp.stack([queries] * axis_size('ctx'), 0), 'ctx', 0, 0)  120 us
    unnamed x11, local copies, waits for them, and re-layouts  67.4 us
    unnamed x2, other arithmetic  54.4 us
    another operation x1, local copies, waits for them, and re-layouts, per_device(): partial_value[None]  36.5 us
    dot_general x1, matrix products, shard_partial(): jnp.einsum('nhgd,khd->hgnk', query_rows, key_block, preferred_element_typ...  33.7 us
    dot_general x1, matrix products, shard_partial(): jnp.einsum('hgnk,khd->nhgd', rounded, value_block, preferred_element_type...  28 us
    reduce_sum x1, other arithmetic, shard_partial(): row_sum = jnp.sum(weights, axis=-1)  21.6 us
  transfers between devices with their start and end apart: 3, of which 2 were waited for; matrix products, arithmetic and copies ran while one was open for 25% of the time, Pallas kernels for 0%

profile of v1, /device:TPU:12, one launch (start us, length us, event | category | flops | bytes accessed | tf_op | source)
XLA Modules:
  0.0 548.9 jit_solution(7672688280537967251)
XLA Ops:
  0.0 0.0 copy-start
  0.0 5.3 stack.2
  5.3 8.9 %all-to-all-start = ((bf16[32,32,4096]{2,1,0:T(8,128)(2,1)}), bf16[32,32,4096]{2,1,0:T(8,128)(2,1)}, u32[]{:S(2)}, u32[]{:S(2)}) async-start(bf16[32,32,4096]{2,1,0:T(8,128)(2,1)} %stack.2), calls=%async_computation | async-start | bytes 16777216 | tf_op jit(solution)/shard_map/all_to_all | solution.py:47
  15.5 0.0 copy-done
  15.5 0.1 copy.41
  15.7 0.1 copy.32
  15.8 0.4 compare_and_fusion
  16.3 119.9 %all-to-all-done = bf16[32,32,4096]{2,1,0:T(8,128)(2,1)} async-done(((bf16[32,32,4096]{2,1,0:T(8,128)(2,1)}), bf16[32,32,4096]{2,1,0:T(8,128)(2,1)}, u32[]{:S(2)}, u32[]{:S(2)}) %all-to-all-start) | async-done | bytes 8388640 | tf_op jit(solution)/shard_map/all_to_all | solution.py:47
  136.1 9.4 %copy.42 = bf16[128,8,32,128]{3,2,1,0:T(8,128)(2,1)} copy(bf16[128,8,32,128]{3,1,2,0:T(8,128)(2,1)} %bitcast.23) | data formatting | bytes 16777216
  145.5 33.7 %fusion.2 = (f32[2,16,1024]{2,1,0:T(8,128)S(1)}, f32[2,512,1024,16]{2,1,3,0:T(8,128)}) fusion(pred[1024,512]{0,1:T(8,128)(4,1)S(1)} %compare_and_fusion, bf16[512,2,128,1]{0,2,3,1:T(8,128)(2,1)S(1)} %bitcast.65, bf16[1024,2,16,128]{3,2,1,0:T(8,128)(2,1)} %bitcast.60), kind=kOutput, calls=%fused_computation.4 | convolution fusion | flops 4345266176 | bytes 76414976 | tf_op jit(solution)/shard_map/nhgd,khd->hgnk/dot_general | solution.py:14
  179.2 21.6 %fusion.1 = f32[2,16,1024]{2,1,0:T(8,128)S(1)} fusion(f32[2,512,1024,16]{2,1,3,0:T(8,128)} %get-tuple-element.10, f32[2,16,1024]{2,1,0:T(8,128)S(1)} %get-tuple-element.9, pred[1024,512]{0,1:T(8,128)(4,1)S(1)} %compare_and_fusion), kind=kLoop, calls=%fused_computation.3 | loop fusion | flops 67076096 | bytes 67895296 | tf_op jit(solution)/shard_map/reduce_sum | solution.py:20
  200.9 0.3 copy.31
  201.2 0.6 broadcast.70
  201.8 1.9 reduce.1
  203.7 0.9 reshape.96
  204.6 13.5 %all-to-all-start.1 = ((f32[128,1,256]{2,1,0:T(1,128)}), f32[128,1,256]{2,1,0:T(1,128)S(1)}, u32[]{:S(2)}, u32[]{:S(2)}) async-start(f32[128,1,256]{2,1,0:T(1,128)} %reshape.96), calls=%async_computation.1 | async-start | bytes 262144 | tf_op jit(solution)/shard_map/all_to_all | solution.py:58
  218.1 28.0 %fusion.6 = bf16[1024,2,16,128]{0,3,2,1:T(8,128)(2,1)} fusion(f32[1024,2,16]{0,2,1:T(8,128)S(1)} %bitcast.67, bf16[512,2,128,1]{0,2,3,1:T(8,128)(2,1)S(1)} %bitcast.69, f32[2,512,1024,16]{2,1,3,0:T(8,128)} %get-tuple-element.10, f32[2,16,1024]{2,1,0:T(8,128)S(1)} %get-tuple-element.9, pred[1024,512]{0,1:T(8,128)(4,1)S(1)} %compare_and_fusion), kind=kOutput, calls=%fused_computation.8 | convolution fusion | flops 4370464768 | bytes 76546048 | tf_op jit(solution)/shard_map/hgnk,khd->nhgd/dot_general | solution.py:22
  246.1 36.5 %copy.34 = bf16[1,1024,4096]{2,0,1:T(2,128)(2,1)} copy(bf16[1,1024,4096]{1,2,0:T(8,128)(2,1)} %bitcast.61) | data formatting | bytes 16777216 | tf_op jit(solution)/shard_map/broadcast_in_dim;reshape | solution.py:56
  282.7 0.5 broadcast.69
  283.2 52.4 %reduce = bf16[1024,4096]{1,0:T(8,128)(2,1)} reduce(bf16[1024,1,4096]{2,1,0:T(2,128)(2,1)} %bitcast.58, bf16[]{:T(256)} %broadcast.69), dimensions={1}, to_apply=%bitcast.48.reduce_sub_computation | reduce | bytes 16777218
  335.6 15.7 %reshape.94 = bf16[128,2,16384]{2,1,0:T(2,128)(2,1)} reshape(bf16[1024,4096]{1,0:T(8,128)(2,1)} %reduce) | data formatting | bytes 16777216
  351.3 0.0 all-to-all-done.1
  351.3 10.2 %all-to-all-start.2 = ((bf16[128,2,16384]{2,1,0:T(2,128)(2,1)}), bf16[128,2,16384]{2,1,0:T(2,128)(2,1)}, u32[]{:S(2)}, u32[]{:S(2)}) async-start(bf16[128,2,16384]{2,1,0:T(2,128)(2,1)} %reshape.94), calls=%async_computation.2 | async-start | bytes 16777216 | tf_op jit(solution)/shard_map/all_to_all | solution.py:55
  361.6 0.9 reduce.2
  362.5 0.9 reshape.97
  363.4 0.1 reduce_max.22
  363.5 0.1 fusion.14
  363.6 121.9 %all-to-all-done.2 = bf16[128,2,16384]{2,1,0:T(2,128)(2,1)} async-done(((bf16[128,2,16384]{2,1,0:T(2,128)(2,1)}), bf16[128,2,16384]{2,1,0:T(2,128)(2,1)}, u32[]{:S(2)}, u32[]{:S(2)}) %all-to-all-start.2) | async-done | bytes 8388640 | tf_op jit(solution)/shard_map/all_to_all | solution.py:55
  485.4 38.4 %reshape.95 = bf16[1024,1,4096]{2,1,0:T(2,128)(2,1)} reshape(bf16[128,2,16384]{2,1,0:T(2,128)(2,1)} %all-to-all-done.2) | data formatting | bytes 16777216
  523.8 18.9 %bitcast_convert_fusion = f32[1,1024,4096]{2,0,1:T(1,128)S(1)} fusion(bf16[1024,1,4096]{2,1,0:T(2,128)(2,1)} %reshape.95), kind=kLoop, calls=%fused_computation.25 | loop fusion | flops 4194304 | bytes 25165824 | tf_op jit(solution)/shard_map/convert_element_type | solution.py:68
  542.7 5.1 multiply_reduce_fusion
  547.8 0.2 fusion.11
  548.0 0.9 copy.49
  (6 shorter events, 0.1 us)
Async XLA Ops:
  0.0 15.5 %copy-start = (bf16[2,512,256]{2,1,0:T(8,128)(2,1)S(1)}, bf16[2,512,256]{2,1,0:T(8,128)(2,1)}, u32[]{:S(2)}) copy-start(bf16[2,512,256]{2,1,0:T(8,128)(2,1)} %param.5) | copy-start | bytes 1572868
  5.3 130.9 %all-to-all-start = ((bf16[32,32,4096]{2,1,0:T(8,128)(2,1)}), bf16[32,32,4096]{2,1,0:T(8,128)(2,1)}, u32[]{:S(2)}, u32[]{:S(2)}) async-start(bf16[32,32,4096]{2,1,0:T(8,128)(2,1)} %stack.2), calls=%async_computation | async-start | bytes 16777216 | tf_op jit(solution)/shard_map/all_to_all | solution.py:47
  204.6 146.7 %all-to-all-start.1 = ((f32[128,1,256]{2,1,0:T(1,128)}), f32[128,1,256]{2,1,0:T(1,128)S(1)}, u32[]{:S(2)}, u32[]{:S(2)}) async-start(f32[128,1,256]{2,1,0:T(1,128)} %reshape.96), calls=%async_computation.1 | async-start | bytes 262144 | tf_op jit(solution)/shard_map/all_to_all | solution.py:58
  351.3 134.1 %all-to-all-start.2 = ((bf16[128,2,16384]{2,1,0:T(2,128)(2,1)}), bf16[128,2,16384]{2,1,0:T(2,128)(2,1)}, u32[]{:S(2)}, u32[]{:S(2)}) async-start(bf16[128,2,16384]{2,1,0:T(2,128)(2,1)} %reshape.94), calls=%async_computation.2 | async-start | bytes 16777216 | tf_op jit(solution)/shard_map/all_to_all | solution.py:55
